TPU v7x, 32 devices: a whole 2x2x4 slice. The times are simulated.
32 devices in a mesh: groups: 2 (over y), panels: 4 (over z), cols: 2 (over x), phase: 2 (over core).
Axes of the slice: x: 2, y: 2, z: 4, core: 2. Of those that a mesh axis runs over, the one named last changes fastest.
Arguments:
- base_points: float32 [3, 512], P(None, ('groups', 'panels', 'cols')), parts along dimension 1, may hold values from -6 to 6
- control_points: float32 [3, 2048], replicated, may hold values from -6 to 6
- morph_weights: float32 [4, 3, 2048], P('groups'), parts along dimension 0, may hold values from -0.15 to 0.15
- connectivity: int32 [3, 1024], P(None, ('groups', 'panels', 'cols')), parts along dimension 1, may hold values from 0 to 255, as said below
- free_flags: int32 [1024], P(('groups', 'panels', 'cols')), parts along dimension 0, may hold values 0 or 1
- station_owner: int32 [1024, 1], P(('groups', 'panels', 'cols')), parts along dimension 0, may hold values from 0 to 7; in each aligned block of 64 rows (0 to 63, 64 to 127, ...) at most 20 rows name the same one
- variant_order: int32 [4], P('groups'), parts along dimension 0, may hold values from 0 to 1, each once
- load_velocity: float32 [64, 3], replicated, may hold values from -5 to 5
Outputs:
- shear: float32 [4, 64, 1024], P(('groups', 'phase'), None, ('panels', 'cols')), parts along dimension 0
- moment: float32 [4, 64, 1024], P(('groups', 'phase'), None, ('panels', 'cols')), parts along dimension 0
There are 2 independent parts, one for each index of `groups`. A program takes and returns all parts, laid end to end along the dimension named above; an argument that names none is the same for every part. Nothing has to cross between parts.
Inputs may be any that keep to these rules, and one draw needn't show every extreme that they name: `connectivity`: the vertices of panel i lie in block i // 64 of 32 consecutive vertices: from (i // 64) * 32 to (i // 64 + 1) * 32 - 1. `station_owner`: among the panels of one device (aligned blocks of 64 panels) no station owner is named more than 20 times. `variant_order`: each variant appears once.
All inputs are finite; a program needn't handle non-finite values. No bound on the sum of `free_flags` on one device may be relied on, other than what follows from the above.
Results may differ from a plain program's by a relative error of at most 0.0015.
Values may be sent and summed in bfloat16 or wider, within the bound.
A program may use at most 64 MiB of HBM per device.

v0:
```python
import math
import jax
import jax.numpy as jnp
from jax import lax
from jax.sharding import PartitionSpec as P

STATIONS = 128
HIGH = lax.Precision.HIGHEST
CORE_SQUARE = 0.0025
SKIN_SQUARE = 0.01


def prefix(shard, axis, combine, identity):
    length, index = (lax.axis_size(axis), lax.axis_index(axis))
    everything = jax.tree.map(lambda part: lax.all_gather(part, axis), shard)
    start = jax.tree.map(
        lambda part, zero: jnp.broadcast_to(jnp.asarray(zero, part.dtype), part.shape),
        shard,
        identity,
    )

    def step(k, before):
        reached = k < index
        new = combine(before, jax.tree.map(lambda part: part[k], everything))
        return jax.tree.map(lambda a, b: jnp.where(reached, a, b), new, before)

    return lax.fori_loop(0, length, step, start)


def panel_shape(moved_points, corner_rows):
    first_corner = jnp.take(moved_points, corner_rows[0], axis=2)
    second_corner = jnp.take(moved_points, corner_rows[1], axis=2)
    third_corner = jnp.take(moved_points, corner_rows[2], axis=2)
    centroid = (first_corner + second_corner + third_corner) / 3.0
    edge_one = second_corner - first_corner
    edge_two = third_corner - first_corner
    cross_x = edge_one[:, 1] * edge_two[:, 2] - edge_one[:, 2] * edge_two[:, 1]
    cross_y = edge_one[:, 2] * edge_two[:, 0] - edge_one[:, 0] * edge_two[:, 2]
    cross_z = edge_one[:, 0] * edge_two[:, 1] - edge_one[:, 1] * edge_two[:, 0]
    area = 0.5 * jnp.stack([cross_x, cross_y, cross_z], axis=1)
    weight = jnp.sqrt(jnp.sum(area * area, axis=1) + SKIN_SQUARE)
    return (centroid, area, weight)


def tile_block(targets, sources, strengths, kernel_scale):
    distance = (
        (targets[:, 0, :, None] - sources[:, 0, None, :]) ** 2
        + (targets[:, 1, :, None] - sources[:, 1, None, :]) ** 2
        + (targets[:, 2, :, None] - sources[:, 2, None, :]) ** 2
    )
    influence = (sources[:, 3, None, :] * kernel_scale * lax.rsqrt(distance + CORE_SQUARE)).astype(
        jnp.bfloat16
    )
    return jnp.einsum("mrn,mkn->mkr", influence, strengths, preferred_element_type=jnp.float32)


def tile_product(carry_sum, targets, sources, strengths, kernel_scale):
    columns = strengths.shape[2]
    block_width = columns
    for candidate in (2048, 1024, 512):
        if columns > candidate and columns % candidate == 0:
            block_width = candidate
            break
    if block_width == columns:
        return carry_sum + tile_block(targets, sources, strengths, kernel_scale)

    def block_step(step_index, running_sum):
        column_start = step_index * block_width
        part_sources = lax.dynamic_slice_in_dim(sources, column_start, block_width, 2)
        part_strengths = lax.dynamic_slice_in_dim(strengths, column_start, block_width, 2)
        return running_sum + tile_block(targets, part_sources, part_strengths, kernel_scale)

    return lax.fori_loop(0, columns // block_width, block_step, carry_sum)


def add_pairs(earlier, later):
    return (earlier[0] + later[0], earlier[1] + later[1])


def shards(
    base_points,
    control_points,
    morph_weights,
    connectivity,
    free_flags,
    station_owner,
    variant_order,
    load_velocity,
):
    owners = lax.axis_size(("panels", "cols"))
    owner_index = lax.axis_index(("panels", "cols"))
    phase_index = lax.axis_index("phase")
    variant_dev = variant_order.shape[0] // lax.axis_size("phase")
    vert_dev = base_points.shape[1]
    pan_dev = connectivity.shape[1]
    load_count = load_velocity.shape[0]
    panels_total = pan_dev * owners
    own_variants = lax.dynamic_slice_in_dim(
        variant_order, phase_index * variant_dev, variant_dev, 0
    )
    picker = (
        own_variants[:, None] == jnp.arange(variant_order.shape[0], dtype=jnp.int32)[None, :]
    ).astype(jnp.float32)
    chosen = jnp.einsum("mv,vac->mac", picker, morph_weights, precision=HIGH)
    distance = (
        (control_points[0][:, None] - base_points[0][None, :]) ** 2
        + (control_points[1][:, None] - base_points[1][None, :]) ** 2
        + (control_points[2][:, None] - base_points[2][None, :]) ** 2
    )
    basis_values = lax.rsqrt(1.0 + distance)
    moved_points = base_points[None] + jnp.einsum(
        "mac,cn->man", chosen, basis_values, precision=HIGH
    )
    local_corners = connectivity - owner_index * vert_dev
    centroid, area, weight = panel_shape(moved_points, local_corners)
    hull_mask = (1 - free_flags).astype(jnp.float32)
    boundary = (
        jnp.einsum("ka,man->mkn", load_velocity, area, precision=HIGH) * hull_mask[None, None, :]
    )
    first_strengths = boundary.astype(jnp.bfloat16)
    kernel_scale = 1.0 / (4.0 * math.pi * math.sqrt(panels_total))
    own_geometry = jnp.concatenate([centroid, weight[:, None, :]], axis=1)
    sources = lax.all_gather(own_geometry, "panels", axis=2, tiled=True)
    row_targets = lax.all_gather(centroid, "cols", axis=2, tiled=True)

    def apply_influence(strengths):
        empty_sum = jnp.zeros((variant_dev, load_count, row_targets.shape[2]), jnp.float32)
        partial_sums = tile_product(
            empty_sum,
            row_targets,
            sources,
            lax.all_gather(strengths, "panels", axis=2, tiled=True),
            kernel_scale,
        )
        return lax.psum_scatter(partial_sums, "cols", scatter_dimension=2, tiled=True)

    induced = apply_influence(first_strengths)
    second_strengths = (first_strengths.astype(jnp.float32) + (boundary - induced)).astype(
        jnp.bfloat16
    )
    pressure = apply_influence(second_strengths)
    panel_force = pressure * (area[:, 2, :] * hull_mask[None, :])[:, None, :]
    force_rows = panel_force.reshape(-1, pan_dev)
    capacity = max(2, 5 * pan_dev // (2 * owners))
    target_owner = station_owner[:, 0]
    panel_order = jnp.arange(pan_dev, dtype=jnp.int32)
    ahead = (target_owner[:, None] == target_owner[None, :]) & (
        panel_order[None, :] < panel_order[:, None]
    )
    slot_rank = jnp.sum(ahead.astype(jnp.int32), axis=1)
    slot_index = target_owner * capacity + slot_rank
    all_slots = jnp.arange(owners * capacity, dtype=jnp.int32)
    placed = slot_index[:, None] == all_slots[None, :]
    send_values = jnp.dot(force_rows, placed.astype(jnp.float32), precision=HIGH)
    station_bins = (owner_index * pan_dev + panel_order) % STATIONS
    send_bins = jnp.max(jnp.where(placed, station_bins[:, None], -1), axis=0)[None, :]
    recv_values, recv_bins = (
        lax.all_to_all(send_values, ("panels", "cols"), split_axis=1, concat_axis=1, tiled=True),
        lax.all_to_all(send_bins, ("panels", "cols"), split_axis=1, concat_axis=1, tiled=True),
    )
    matches = (recv_bins[0][:, None] == jnp.arange(STATIONS, dtype=jnp.int32)[None, :]).astype(
        jnp.float32
    )
    station_loads = jnp.dot(recv_values, matches, precision=HIGH)
    station_place = (owner_index * STATIONS + jnp.arange(STATIONS, dtype=jnp.int32)).astype(
        jnp.float32
    ) / (STATIONS * owners)
    placed_loads = station_loads * station_place[None, :]
    own_total = jnp.sum(station_loads, axis=1)
    own_arm = jnp.sum(placed_loads, axis=1)
    zero_row = jnp.zeros_like(own_total)
    prior_total, prior_arm = prefix(
        (own_total, own_arm), ("panels", "cols"), add_pairs, (zero_row, zero_row)
    )
    station_rank = jnp.arange(STATIONS, dtype=jnp.int32)
    inclusive = (station_rank[:, None] <= station_rank[None, :]).astype(jnp.float32)
    strict = (station_rank[:, None] < station_rank[None, :]).astype(jnp.float32)
    running = prior_total[:, None] + jnp.dot(station_loads, inclusive, precision=HIGH)
    earlier = prior_total[:, None] + jnp.dot(station_loads, strict, precision=HIGH)
    moment_arm = prior_arm[:, None] + jnp.dot(placed_loads, strict, precision=HIGH)
    inv_root = 1.0 / math.sqrt(panels_total)
    shear = (running * inv_root).reshape(variant_dev, load_count, STATIONS)
    moment = ((station_place[None, :] * earlier - moment_arm) * inv_root).reshape(
        variant_dev, load_count, STATIONS
    )
    return (shear, moment)


def solution(mesh):
    return jax.shard_map(
        shards,
        mesh=mesh,
        in_specs=(
            P(None, ("groups", "panels", "cols")),
            P(),
            P("groups", None, None),
            P(None, ("groups", "panels", "cols")),
            P(("groups", "panels", "cols")),
            P(("groups", "panels", "cols"), None),
            P("groups"),
            P(),
        ),
        out_specs=(
            P(("groups", "phase"), None, ("panels", "cols")),
            P(("groups", "phase"), None, ("panels", "cols")),
        ),
        check_vma=False,
    )
```

profile of v0, /device:TPU:0, one launch (start us, length us, event | category | flops | bytes accessed | tf_op | source)
XLA Modules:
  0.0 130.9 jit_solution(7332633443924360634)
XLA Ops:
  7.2 0.9 fusion.63
  8.2 0.6 copy-done.4
  8.8 0.6 dynamic_slice.17
  9.4 0.9 fusion.48
  10.3 0.4 convolution_add_fusion.3
  10.8 0.7 copy-done.1
  11.5 0.6 gather_fusion.2
  12.1 0.6 gather_fusion
  12.7 0.6 gather_fusion.1
  13.4 0.2 fusion.60
  14.0 0.1 copy.52
  14.1 5.5 %all_gather.26 = f32[1,3,128]{1,2,0:T(8,128)S(1)} all-gather(f32[1,3,64]{1,2,0:T(8,128)S(1)} %get-tuple-element.175), channel_id=1, replica_groups=mesh['groups'=2,'panels'=4,'cols'=2,'phase'=2] {'cols'}, dimensions={2}, use_global_device_ids=true | all-gather | bytes 2304 | tf_op jit(solution)/shard_map/all_gather | solution.py:124
  19.6 14.1 %all_gather.25 = f32[1,4,256]{1,0,2:T(1,128)S(1)} all-gather(f32[1,4,64]{1,0,2:T(1,128)S(1)} %bitcast.124), channel_id=1, replica_groups=mesh['groups'=2,'panels'=4,'cols'=2,'phase'=2] {'panels'}, dimensions={2}, use_global_device_ids=true | all-gather | bytes 5120 | tf_op jit(solution)/shard_map/all_gather | solution.py:123
  33.8 3.3 %fusion.25 = (f32[256]{0:T(256)S(1)}, f32[256]{0:T(256)S(1)}, f32[256]{0:T(256)S(1)}, f32[256]{0:T(256)S(1)}) fusion(f32[1,4,256]{1,0,2:T(1,128)S(1)} %all_gather.25), kind=kLoop, calls=%fused_computation.44 | loop fusion | flops 256 | bytes 8192 | tf_op jit(solution)/shard_map/mul | solution.py:51
  37.1 0.7 copy-done.3
  37.8 0.2 fusion.64
  38.1 13.2 %all_gather.24 = bf16[1,64,256]{1,2,0:T(8,128)(2,1)S(1)} all-gather(bf16[1,64,64]{1,2,0:T(8,128)(2,1)S(1)} %get-tuple-element.192), channel_id=1, replica_groups=mesh['groups'=2,'panels'=4,'cols'=2,'phase'=2] {'panels'}, dimensions={2}, use_global_device_ids=true | all-gather | bytes 40960 | tf_op jit(solution)/shard_map/all_gather | solution.py:132
  51.3 0.2 slice_reduce_fusion.5
  51.5 0.9 convolution_bitcast_fusion.1
  52.4 0.6 copy-done.5
  53.1 0.2 convert_reduce_fusion
  53.3 0.1 select_reduce_fusion
  53.4 0.7 all_to_all.14
  54.1 5.7 %all-to-all-start.1 = ((s32[1,8,20]{2,0,1:T(1,128)}), s32[1,8,20]{2,0,1:T(1,128)S(1)}, u32[]{:S(2)}, u32[]{:S(2)}) async-start(s32[1,8,20]{2,0,1:T(1,128)} %all_to_all.14), calls=%async_computation.2 | async-start | bytes 8192 | tf_op jit(solution)/shard_map/all_to_all | solution.py:159
  59.8 0.6 copy-done.7
  60.5 0.7 dynamic-slice
  61.8 1.9 %reduce-scatter.5.cloned.1.call-done = f32[1,64,64]{1,2,0:T(8,128)} async-done(((f32[1,64,128]{1,2,0:T(8,128)}), f32[1,64,64]{1,2,0:T(8,128)}) %reduce-scatter.5.cloned.1.call-update) | async-done | bytes 16400 | tf_op jit(solution)/shard_map/reduce_scatter | solution.py:135
  63.7 0.8 add_convert_fusion
  64.4 13.2 %all_gather.27 = bf16[1,64,256]{1,2,0:T(8,128)(2,1)S(1)} all-gather(bf16[1,64,64]{1,2,0:T(8,128)(2,1)S(1)} %add_convert_fusion), channel_id=1, replica_groups=mesh['groups'=2,'panels'=4,'cols'=2,'phase'=2] {'panels'}, dimensions={2}, use_global_device_ids=true | all-gather | bytes 40960 | tf_op jit(solution)/shard_map/all_gather | solution.py:132
  77.7 0.9 convolution_bitcast_fusion
  78.6 10.1 %reduce-scatter.7.cloned.1.call-done = f32[64,64]{1,0:T(8,128)} async-done(((f32[128,64]{1,0:T(8,128)}), f32[64,64]{1,0:T(8,128)}) %reduce-scatter.7.cloned.1.call-update) | async-done | bytes 16400
  88.6 0.8 copy.58
  89.5 0.3 fusion.65
  89.7 0.7 reshape.458
  90.4 4.6 %all-to-all-start = ((f32[8,1,1280]{2,1,0:T(1,128)}), f32[8,1,1280]{2,1,0:T(1,128)S(1)}, u32[]{:S(2)}, u32[]{:S(2)}) async-start(f32[8,1,1280]{2,1,0:T(1,128)} %reshape.458), calls=%async_computation.1 | async-start | bytes 81920 | tf_op jit(solution)/shard_map/all_to_all | solution.py:158
  95.1 0.5 broadcast.246
  95.6 0.7 reduce.21
  96.3 5.5 %all-to-all-done = f32[8,1,1280]{2,1,0:T(1,128)S(1)} async-done(((f32[8,1,1280]{2,1,0:T(1,128)}), f32[8,1,1280]{2,1,0:T(1,128)S(1)}, u32[]{:S(2)}, u32[]{:S(2)}) %all-to-all-start) | async-done | bytes 40992 | tf_op jit(solution)/shard_map/all_to_all | solution.py:158
  101.8 0.5 broadcast.247
  102.3 0.7 reduce.25
  103.2 0.4 multiply_reduce_fusion
  103.6 0.2 dynamic-update-slice
  103.8 0.2 dynamic-update-slice.1
  104.0 17.8 %all-reduce.2 = (f32[512]{0:T(512)S(1)}, f32[512]{0:T(512)S(1)}) all-reduce(f32[512]{0:T(512)S(1)} %dynamic-update-slice, f32[512]{0:T(512)S(1)} %dynamic-update-slice.1), channel_id=2, replica_groups=mesh['groups'=2,'panels'=4,'cols'=2,'phase'=2] {'panels','cols'}, use_global_device_ids=true, to_apply=%add | all-reduce | flops 1024 | bytes 8192
  122.0 0.3 while.16
  122.3 0.2 fusion.3
  122.5 0.8 fusion.5
  123.3 0.8 fusion.2
  (52 shorter events, 1.2 us)
Async XLA Ops:
  7.2 2.2 %copy-start = (f32[2,3,2048]{2,0,1:T(2,128)S(1)}, f32[2,3,2048]{2,0,1:T(2,128)}, u32[]{:S(2)}) copy-start(f32[2,3,2048]{2,0,1:T(2,128)} %param.14) | copy-start | bytes 147460
  7.2 56.5 %reduce-scatter.5.cloned.1.call-start = ((), (), s32[]{:S(2)}) async-start(), calls=%async_computation.4 | async-start | bytes 98304 | tf_op jit(solution)/shard_map/reduce_scatter | solution.py:135
  7.2 0.9 copy-start.2
  8.2 0.7 copy-start.4
  10.8 0.7 copy-start.1
  33.8 3.3 %copy-start.6 = (s32[64]{0:T(128)S(1)}, s32[64]{0:T(128)}, u32[]{:S(2)}) copy-start(s32[64]{0:T(128)} %param.16) | copy-start | bytes 772
  37.1 0.7 copy-start.3
  52.4 0.7 copy-start.5
  54.1 36.4 %all-to-all-start.1 = ((s32[1,8,20]{2,0,1:T(1,128)}), s32[1,8,20]{2,0,1:T(1,128)S(1)}, u32[]{:S(2)}, u32[]{:S(2)}) async-start(s32[1,8,20]{2,0,1:T(1,128)} %all_to_all.14), calls=%async_computation.2 | async-start | bytes 8192 | tf_op jit(solution)/shard_map/all_to_all | solution.py:159
  59.7 28.9 %reduce-scatter.7.cloned.1.call-start = ((), (), s32[]{:S(2)}) async-start(), calls=%async_computation.5 | async-start | bytes 98304
  59.8 0.7 copy-start.7
  90.4 11.4 %all-to-all-start = ((f32[8,1,1280]{2,1,0:T(1,128)}), f32[8,1,1280]{2,1,0:T(1,128)S(1)}, u32[]{:S(2)}, u32[]{:S(2)}) async-start(f32[8,1,1280]{2,1,0:T(1,128)} %reshape.458), calls=%async_computation.1 | async-start | bytes 81920 | tf_op jit(solution)/shard_map/all_to_all | solution.py:158
Sparse Core Ops, SparseCore 0:
  52.5 11.1 reduce-scatter.4
  78.7 9.9 reduce-scatter.6
where the time goes:
time: 131 us
  blocking collectives  63.9 us (49%)
  waiting for transfers between devices  17.4 us (13%)
  between operations  15 us (11%)
  local copies, waits for them, and re-layouts  11.9 us (9%)
  starting transfers between devices  10.4 us (8%)
  other arithmetic  6.43 us (5%)
  matrix products  5.69 us (4%)
    all_gather x2, blocking collectives, apply_influence(): lax.all_gather(strengths, 'panels', axis=2, tiled=True)  26.4 us
    unnamed x1, blocking collectives  17.8 us
    all_gather x1, blocking collectives, shards(): sources = lax.all_gather(own_geometry, 'panels', axis=2, tiled=True)  14.1 us
    unnamed x3, waiting for transfers between devices  10.1 us
    unnamed x24, local copies, waits for them, and re-layouts  6.08 us
    all_to_all x1, starting transfers between devices, shards(): lax.all_to_all(send_bins, ('panels', 'cols'), split_axis=1, concat_axis=1...  5.67 us
    all_gather x1, blocking collectives, shards(): row_targets = lax.all_gather(centroid, 'cols', axis=2, tiled=True)  5.51 us
    all_to_all x1, waiting for transfers between devices, shards(): lax.all_to_all(send_values, ('panels', 'cols'), split_axis=1, concat_axis...  5.47 us
  transfers between devices with their start and end apart: 4, of which 3 were waited for; matrix products, arithmetic and copies ran while one was open for 4% of the time, Pallas kernels for 0%

commit v1 on v0

--- a/solution.py
+++ b/solution.py
@@ -1,3 +1,4 @@
+import functools
 import math
 import jax
 import jax.numpy as jnp
@@ -8,6 +9,28 @@
 HIGH = lax.Precision.HIGHEST
 CORE_SQUARE = 0.0025
 SKIN_SQUARE = 0.01
+
+
+def mark_joints(mine, axis_id):
+    value_now, tile_out, item_now = (lax.axis_size(axis_id), lax.axis_index(axis_id), mine.shape[2])
+    passed, m_next = (mine, 1)
+    while m_next < value_now:
+        passed = jnp.concatenate(
+            [
+                passed,
+                lax.ppermute(
+                    passed,
+                    axis_id,
+                    tuple(((at, (at - m_next) % value_now) for at in range(value_now))),
+                ),
+            ],
+            2,
+        )
+        m_next = 2 * m_next
+    return jnp.roll(passed, tile_out * item_now, 2)
+
+
+search_unit = functools.partial(mark_joints, axis_id="panels")
 
 
 def prefix(shard, axis, combine, identity):
@@ -126,11 +149,7 @@
     def apply_influence(strengths):
         empty_sum = jnp.zeros((variant_dev, load_count, row_targets.shape[2]), jnp.float32)
         partial_sums = tile_product(
-            empty_sum,
-            row_targets,
-            sources,
-            lax.all_gather(strengths, "panels", axis=2, tiled=True),
-            kernel_scale,
+            empty_sum, row_targets, sources, search_unit(strengths), kernel_scale
         )
         return lax.psum_scatter(partial_sums, "cols", scatter_dimension=2, tiled=True)
 

time: 131 us -> 125 us (0.954)
  blocking collectives: 63.9 us -> 35.9 us
  waiting for transfers between devices: 17.4 us -> 29.2 us
  starting transfers between devices: 10.4 us -> 19.9 us
    all_gather x2 -> x0, blocking collectives: 26.4 us -> none  [apply_influence(): lax.all_gather(strengths, 'panels', axis=2, tiled=True)]
    ppermute x0 -> x4, starting transfers between devices: none -> 11.9 us  [mark_joints(): lax.ppermute(passed, axis_id, tuple(((at, (at - m_next) % value_now) for...]
    unnamed x3 -> x4, waiting for transfers between devices: 10.1 us -> 19.9 us
    ppermute x0 -> x4, waiting for transfers between devices: none -> 3.83 us  [mark_joints(): lax.ppermute(passed, axis_id, tuple(((at, (at - m_next) % value_now) for...]
    all_to_all x1, starting transfers between devices: 5.67 us -> 3.31 us  [shards(): lax.all_to_all(send_bins, ('panels', 'cols'), split_axis=1, concat_axis=1...]
    reduce_scatter x1 -> x0, waiting for transfers between devices: 1.86 us -> none  [apply_influence(): lax.psum_scatter(partial_sums, 'cols', scatter_dimension=2, tiled=True)]
    unnamed x24 -> x25, local copies, waits for them, and re-layouts: 6.08 us -> 7 us
  transfers between devices with their start and end apart: 4 -> 8, of which waited for: 3 -> 4; matrix products, arithmetic and copies ran while one was open for 4% -> 7% of each run, Pallas kernels for 0% -> 0%
where the time goes in v1:
time: 125 us
  blocking collectives  35.9 us (29%)
  waiting for transfers between devices  29.2 us (23%)
  starting transfers between devices  19.9 us (16%)
  between operations  15 us (12%)
  local copies, waits for them, and re-layouts  12.8 us (10%)
  matrix products  5.87 us (5%)
  other arithmetic  5.84 us (5%)
    unnamed x4, waiting for transfers between devices  19.9 us
    unnamed x1, blocking collectives  17.8 us
    all_gather x1, blocking collectives, shards(): sources = lax.all_gather(own_geometry, 'panels', axis=2, tiled=True)  13.5 us
    ppermute x4, starting transfers between devices, mark_joints(): lax.ppermute(passed, axis_id, tuple(((at, (at - m_next) % value_now) for...  11.9 us
    unnamed x25, local copies, waits for them, and re-layouts  7 us
    all_to_all x1, waiting for transfers between devices, shards(): lax.all_to_all(send_values, ('panels', 'cols'), split_axis=1, concat_axis...  5.47 us
    all_to_all x1, starting transfers between devices, shards(): lax.all_to_all(send_values, ('panels', 'cols'), split_axis=1, concat_axis...  4.61 us
    all_gather x1, blocking collectives, shards(): row_targets = lax.all_gather(centroid, 'cols', axis=2, tiled=True)  4.58 us
  transfers between devices with their start and end apart: 8, of which 4 were waited for; matrix products, arithmetic and copies ran while one was open for 7% of the time, Pallas kernels for 0%

profile of v1, /device:TPU:0, one launch (start us, length us, event | category | flops | bytes accessed | tf_op | source)
XLA Modules:
  0.0 124.7 jit_solution(1848303088340533278)
XLA Ops:
  7.2 0.7 copy-done.2
  7.9 0.9 fusion.81
  8.8 0.6 copy-done.4
  9.5 0.6 dynamic_slice.20
  10.1 0.9 fusion.64
  10.9 0.4 convolution_add_fusion.3
  11.5 0.7 copy-done.1
  12.2 0.6 gather_fusion
  12.8 0.6 gather_fusion.2
  13.4 0.6 gather_fusion.1
  14.2 0.2 fusion.78
  14.4 0.7 copy-done.3
  15.1 0.2 fusion.82
  15.3 5.1 %collective-permute-start = (bf16[1,64,64]{2,1,0:T(8,128)(2,1)S(1)}, bf16[1,64,64]{2,1,0:T(8,128)(2,1)S(1)}, u32[]{:S(2)}, u32[]{:S(2)}) collective-permute-start(bf16[1,64,64]{2,1,0:T(8,128)(2,1)S(1)} %get-tuple-element.193), channel_id=1, source_target_pairs={{0,12},{4,0},{8,4},{12,8},{1,13},{5,1},{9,5},{13,9},{2,14},{6,2},{... | collective-permute-start | bytes 24584 | tf_op jit(solution)/shard_map/ppermute | solution.py:21
  20.5 0.2 convert_reduce_fusion
  21.1 13.5 %all_gather.18 = f32[1,4,256]{1,0,2:T(1,128)S(1)} all-gather(f32[1,4,64]{1,0,2:T(1,128)S(1)} %bitcast.132), channel_id=1, replica_groups=mesh['groups'=2,'panels'=4,'cols'=2,'phase'=2] {'panels'}, dimensions={2}, use_global_device_ids=true | all-gather | bytes 5120 | tf_op jit(solution)/shard_map/all_gather | solution.py:146
  34.6 3.3 %fusion.25 = (f32[256]{0:T(256)S(1)}, f32[256]{0:T(256)S(1)}, f32[256]{0:T(256)S(1)}, f32[256]{0:T(256)S(1)}) fusion(f32[1,4,256]{1,0,2:T(1,128)S(1)} %all_gather.18), kind=kLoop, calls=%fused_computation.44 | loop fusion | flops 256 | bytes 8192 | tf_op jit(solution)/shard_map/mul | solution.py:74
  37.9 4.6 %all_gather.19 = f32[1,3,128]{1,2,0:T(8,128)S(1)} all-gather(f32[1,3,64]{1,2,0:T(8,128)S(1)} %get-tuple-element.176), channel_id=1, replica_groups=mesh['groups'=2,'panels'=4,'cols'=2,'phase'=2] {'cols'}, dimensions={2}, use_global_device_ids=true | all-gather | bytes 2304 | tf_op jit(solution)/shard_map/all_gather | solution.py:147
  42.6 0.6 collective-permute-start.1
  43.2 0.2 slice_reduce_fusion.5
  43.4 3.8 %collective-permute-done.1 = bf16[1,64,128]{2,1,0:T(8,128)(2,1)S(1)} collective-permute-done((bf16[1,64,128]{2,1,0:T(8,128)(2,1)S(1)}, bf16[1,64,128]{2,1,0:T(8,128)(2,1)S(1)}, u32[]{:S(2)}, u32[]{:S(2)}) %collective-permute-start.1) | collective-permute-done | bytes 16416 | tf_op jit(solution)/shard_map/ppermute | solution.py:21
  47.2 1.0 convolution_bitcast_fusion.1
  48.3 8.4 %reduce-scatter.7.cloned.1.call-done = f32[64,64]{1,0:T(8,128)} async-done(((f32[128,64]{1,0:T(8,128)}), f32[64,64]{1,0:T(8,128)}) %reduce-scatter.7.cloned.1.call-update) | async-done | bytes 16400
  56.7 0.8 copy.51
  57.5 3.4 %collective-permute-start.2 = (bf16[1,64,64]{2,1,0:T(8,128)(2,1)S(1)}, bf16[1,64,64]{2,1,0:T(8,128)(2,1)S(1)}, u32[]{:S(2)}, u32[]{:S(2)}) collective-permute-start(bf16[1,64,64]{2,1,0:T(8,128)(2,1)S(1)} %add_convert_fusion), channel_id=1, source_target_pairs={{0,12},{4,0},{8,4},{12,8},{1,13},{5,1},{9,5},{13,9},{2,14},{6,2},{... | collective-permute-start | bytes 24584 | tf_op jit(solution)/shard_map/ppermute | solution.py:21
  61.0 0.7 all_to_all.14
  61.7 3.3 %all-to-all-start.1 = ((s32[1,8,20]{2,0,1:T(1,128)}), s32[1,8,20]{2,0,1:T(1,128)S(1)}, u32[]{:S(2)}, u32[]{:S(2)}) async-start(s32[1,8,20]{2,0,1:T(1,128)} %all_to_all.14), calls=%async_computation.1 | async-start | bytes 8192 | tf_op jit(solution)/shard_map/all_to_all | solution.py:178
  65.2 2.8 %collective-permute-start.3 = (bf16[1,64,128]{2,1,0:T(8,128)(2,1)S(1)}, bf16[1,64,128]{2,1,0:T(8,128)(2,1)S(1)}, u32[]{:S(2)}, u32[]{:S(2)}) collective-permute-start(bf16[1,64,128]{2,1,0:T(8,128)(2,1)S(1)} %pad_maximum_fusion.2), channel_id=1, source_target_pairs={{0,8},{4,12},{8,0},{12,4},{1,9},{5,13},{9,1},{13,5},{2,10},{6,14},... | collective-permute-start | bytes 49160 | tf_op jit(solution)/shard_map/ppermute | solution.py:21
  68.0 0.7 copy-done.7
  68.6 0.7 dynamic-slice
  70.0 1.0 convolution_bitcast_fusion
  71.0 11.4 %reduce-scatter.9.cloned.1.call-done = f32[64,64]{1,0:T(8,128)} async-done(((f32[128,64]{1,0:T(8,128)}), f32[64,64]{1,0:T(8,128)}) %reduce-scatter.9.cloned.1.call-update) | async-done | bytes 16400
  82.4 0.8 copy.53
  83.3 0.3 fusion.83
  83.5 0.7 reshape.460
  84.2 4.6 %all-to-all-start = ((f32[8,1,1280]{2,1,0:T(1,128)}), f32[8,1,1280]{2,1,0:T(1,128)S(1)}, u32[]{:S(2)}, u32[]{:S(2)}) async-start(f32[8,1,1280]{2,1,0:T(1,128)} %reshape.460), calls=%async_computation | async-start | bytes 81920 | tf_op jit(solution)/shard_map/all_to_all | solution.py:177
  88.9 0.5 broadcast.247
  89.4 0.7 reduce.21
  90.1 5.5 %all-to-all-done = f32[8,1,1280]{2,1,0:T(1,128)S(1)} async-done(((f32[8,1,1280]{2,1,0:T(1,128)}), f32[8,1,1280]{2,1,0:T(1,128)S(1)}, u32[]{:S(2)}, u32[]{:S(2)}) %all-to-all-start) | async-done | bytes 40992 | tf_op jit(solution)/shard_map/all_to_all | solution.py:177
  95.6 0.5 broadcast.248
  96.1 0.7 reduce.25
  96.9 0.4 multiply_reduce_fusion
  97.3 0.2 dynamic-update-slice
  97.6 0.2 dynamic-update-slice.1
  97.8 17.8 %all-reduce.2 = (f32[512]{0:T(512)S(1)}, f32[512]{0:T(512)S(1)}) all-reduce(f32[512]{0:T(512)S(1)} %dynamic-update-slice, f32[512]{0:T(512)S(1)} %dynamic-update-slice.1), channel_id=2, replica_groups=mesh['groups'=2,'panels'=4,'cols'=2,'phase'=2] {'panels','cols'}, use_global_device_ids=true, to_apply=%add | all-reduce | flops 1024 | bytes 8192
  115.8 0.3 while.16
  116.1 0.8 fusion.5
  117.0 0.8 fusion.2
  (61 shorter events, 1.8 us)
Async XLA Ops:
  7.2 2.9 %copy-start = (f32[2,3,2048]{2,0,1:T(2,128)S(1)}, f32[2,3,2048]{2,0,1:T(2,128)}, u32[]{:S(2)}) copy-start(f32[2,3,2048]{2,0,1:T(2,128)} %param.16) | copy-start | bytes 147460
  7.2 49.5 %reduce-scatter.7.cloned.1.call-start = ((), (), s32[]{:S(2)}) async-start(), calls=%async_computation.4 | async-start | bytes 98304
  7.2 0.7 copy-start.2
  8.8 0.7 copy-start.4
  11.5 0.7 copy-start.1
  13.4 0.7 copy-start.6
  14.4 0.7 copy-start.3
  15.3 5.1 %copy-start.5 = (s32[64,1]{0,1:T(1,128)S(1)}, s32[64,1]{0,1:T(1,128)}, u32[]{:S(2)}) copy-start(s32[64,1]{0,1:T(1,128)} %param.19) | copy-start | bytes 772
  15.3 27.2 %collective-permute-start = (bf16[1,64,64]{2,1,0:T(8,128)(2,1)S(1)}, bf16[1,64,64]{2,1,0:T(8,128)(2,1)S(1)}, u32[]{:S(2)}, u32[]{:S(2)}) collective-permute-start(bf16[1,64,64]{2,1,0:T(8,128)(2,1)S(1)} %get-tuple-element.193), channel_id=1, source_target_pairs={{0,12},{4,0},{8,4},{12,8},{1,13},{5,1},{9,5},{13,9},{2,14},{6,2},{... | collective-permute-start | bytes 24584 | tf_op jit(solution)/shard_map/ppermute | solution.py:21
  42.6 4.6 %collective-permute-start.1 = (bf16[1,64,128]{2,1,0:T(8,128)(2,1)S(1)}, bf16[1,64,128]{2,1,0:T(8,128)(2,1)S(1)}, u32[]{:S(2)}, u32[]{:S(2)}) collective-permute-start(bf16[1,64,128]{2,1,0:T(8,128)(2,1)S(1)} %pad_maximum_fusion.1), channel_id=1, source_target_pairs={{0,8},{4,12},{8,0},{12,4},{1,9},{5,13},{9,1},{13,5},{2,10},{6,14},... | collective-permute-start | bytes 49160 | tf_op jit(solution)/shard_map/ppermute | solution.py:21
  57.5 7.5 %collective-permute-start.2 = (bf16[1,64,64]{2,1,0:T(8,128)(2,1)S(1)}, bf16[1,64,64]{2,1,0:T(8,128)(2,1)S(1)}, u32[]{:S(2)}, u32[]{:S(2)}) collective-permute-start(bf16[1,64,64]{2,1,0:T(8,128)(2,1)S(1)} %add_convert_fusion), channel_id=1, source_target_pairs={{0,12},{4,0},{8,4},{12,8},{1,13},{5,1},{9,5},{13,9},{2,14},{6,2},{... | collective-permute-start | bytes 24584 | tf_op jit(solution)/shard_map/ppermute | solution.py:21
  61.7 22.5 %all-to-all-start.1 = ((s32[1,8,20]{2,0,1:T(1,128)}), s32[1,8,20]{2,0,1:T(1,128)S(1)}, u32[]{:S(2)}, u32[]{:S(2)}) async-start(s32[1,8,20]{2,0,1:T(1,128)} %all_to_all.14), calls=%async_computation.1 | async-start | bytes 8192 | tf_op jit(solution)/shard_map/all_to_all | solution.py:178
  65.0 17.4 %reduce-scatter.9.cloned.1.call-start = ((), (), s32[]{:S(2)}) async-start(), calls=%async_computation.5 | async-start | bytes 98304
  65.2 4.8 %collective-permute-start.3 = (bf16[1,64,128]{2,1,0:T(8,128)(2,1)S(1)}, bf16[1,64,128]{2,1,0:T(8,128)(2,1)S(1)}, u32[]{:S(2)}, u32[]{:S(2)}) collective-permute-start(bf16[1,64,128]{2,1,0:T(8,128)(2,1)S(1)} %pad_maximum_fusion.2), channel_id=1, source_target_pairs={{0,8},{4,12},{8,0},{12,4},{1,9},{5,13},{9,1},{13,5},{2,10},{6,14},... | collective-permute-start | bytes 49160 | tf_op jit(solution)/shard_map/ppermute | solution.py:21
  68.0 0.7 copy-start.7
  84.2 11.3 %all-to-all-start = ((f32[8,1,1280]{2,1,0:T(1,128)}), f32[8,1,1280]{2,1,0:T(1,128)S(1)}, u32[]{:S(2)}, u32[]{:S(2)}) async-start(f32[8,1,1280]{2,1,0:T(1,128)} %reshape.460), calls=%async_computation | async-start | bytes 81920 | tf_op jit(solution)/shard_map/all_to_all | solution.py:177
Sparse Core Ops, SparseCore 0:
  48.4 8.2 reduce-scatter.6
  71.1 11.2 reduce-scatter.8
